TPU v7x, 32 devices: a whole 2x2x4 slice. The times are simulated.
32 devices in a mesh: row: 16 (over z, x, core), col: 2 (over y).
Axes of the slice: x: 2, y: 2, z: 4, core: 2. Of those that a mesh axis runs over, the one named last changes fastest.
Arguments:
- tiles: bfloat16 [16, 2, 256, 128, 128], P('row', 'col'), may hold values from 0 to 0.00064849854
- tile_row: int32 [16, 2, 256], P('row', 'col'), may hold values from 0 to 16, as said below
- tile_col: int32 [16, 2, 256], P('row', 'col'), may hold values from 0 to 128, as said below
- right_vecs: bfloat16 [256, 32, 128], P(('row', 'col')), may hold values from -6 to 6
- left_vecs: bfloat16 [256, 32, 128], P(('row', 'col')), may hold values from -6 to 6
Outputs:
- right_next: float32 [256, 32, 128], P(('row', 'col'))
- left_next: float32 [256, 32, 128], P(('row', 'col'))
- gram: float32 [32, 32], replicated
Inputs may be any that keep to these rules, and one draw needn't show every extreme that they name: Value 16 marks an empty slot; a slot is empty in tile_row exactly when it is empty in tile_col; live slots come first on each device; each device has 128 to 256 live slots and some device has all 256 live. `tile_col`: value 128 marks an empty slot, in the same slots as tile_row.
All inputs are finite; a program needn't handle non-finite values.
Results may differ from a plain program's by a relative error of at most 0.0003.
Values may be sent and summed in bfloat16 or wider, within the bound.
A program may use at most 64 MiB of HBM per device.

v0:
```python
import jax
import jax.numpy as jnp
from jax import lax
from jax.sharding import PartitionSpec as P


def per_device(tiles, tile_row, tile_col, right_vecs, left_vecs):
    highest = lax.Precision.HIGHEST
    local_tiles = tiles[0, 0]
    slot_rows = tile_row[0, 0]
    slot_cols = tile_col[0, 0]
    piece_tiles = right_vecs.shape[0]
    block_rows = piece_tiles * lax.axis_size("col")
    block_cols = piece_tiles * lax.axis_size("row")
    box_count = block_rows * lax.axis_size("row") * right_vecs.shape[2]
    column_vecs = lax.all_gather(right_vecs, "row", axis=0, tiled=True)
    chosen_right = jnp.take(column_vecs, jnp.minimum(slot_cols, block_cols - 1), axis=0)
    forward = jnp.einsum(
        "sef,skf->ske", local_tiles, chosen_right, preferred_element_type=jnp.float32
    )
    row_select = (
        lax.broadcasted_iota(jnp.int32, (block_rows, slot_rows.shape[0]), 0) == slot_rows[None, :]
    ).astype(jnp.float32)
    partial_right = jnp.einsum("rs,ske->rke", row_select, forward, precision=highest)
    row_vecs = lax.all_gather(left_vecs, "col", axis=0, tiled=True)
    chosen_left = jnp.take(row_vecs, jnp.minimum(slot_rows, block_rows - 1), axis=0)
    backward = jnp.einsum(
        "sef,ske->skf", local_tiles, chosen_left, preferred_element_type=jnp.float32
    )
    local_gram = jnp.einsum(
        "tke,tle->kl", row_vecs.astype(jnp.float32), partial_right, precision=highest
    )
    gram = lax.psum(local_gram, ("row", "col")) * box_count ** (-0.5)
    right_sums = lax.psum_scatter(partial_right, "col", scatter_dimension=0, tiled=True)
    column_total = jax.ops.segment_sum(backward, slot_cols, num_segments=block_cols)
    left_sums = lax.psum_scatter(column_total, "row", scatter_dimension=0, tiled=True)
    right_next = right_sums - jnp.einsum(
        "tke,kl->tle", right_vecs.astype(jnp.float32), gram, precision=highest
    )
    left_next = left_sums - jnp.einsum(
        "tle,kl->tke", left_vecs.astype(jnp.float32), gram, precision=highest
    )
    return (right_next, left_next, gram)


def solution(mesh):
    placed = (
        P("row", "col", None, None, None),
        P("row", "col", None),
        P("row", "col", None),
        P(("row", "col"), None, None),
        P(("row", "col"), None, None),
    )
    return jax.shard_map(
        per_device,
        mesh=mesh,
        in_specs=placed,
        out_specs=(P(("row", "col"), None, None), P(("row", "col"), None, None), P()),
        check_vma=False,
    )
```

profile of v0, /device:TPU:0, one launch (start us, length us, event | category | flops | bytes accessed | tf_op | source)
XLA Modules:
  0.0 168.6 jit_solution(17989274664771482361)
XLA Ops:
  7.2 0.0 all-gather.2.cloned.1.call-start
  7.2 0.7 all-gather.2.cloned.1.call-update
  7.9 0.0 reduce-scatter.3.cloned.1.call-start
  7.9 6.2 %all_gather.7 = bf16[16,32,128]{2,1,0:T(8,128)(2,1)S(1)} all-gather(bf16[8,32,128]{2,1,0:T(8,128)(2,1)} %param.9), channel_id=1, replica_groups=mesh['row'=16,'col'=2] {'col'}, dimensions={0}, use_global_device_ids=true | all-gather | bytes 196608 | tf_op jit(solution)/shard_map/all_gather | solution.py:25
  14.1 0.7 compare_select_fusion
  14.8 0.0 copy-start.4
  14.8 0.0 copy-start.5
  14.8 1.0 gather_fusion.1
  15.8 0.0 copy-done.4
  15.9 0.0 copy-done.5
  15.9 34.8 %all-gather.2.cloned.1.call-done = bf16[128,32,128]{2,1,0:T(8,128)(2,1)} async-done(((bf16[8,32,128]{2,1,0:T(8,128)(2,1)}), bf16[128,32,128]{2,1,0:T(8,128)(2,1)}) %all-gather.2.cloned.1.call-update) | async-done | bytes 1048592 | tf_op jit(solution)/shard_map/all_gather | solution.py:16
  50.7 3.4 %gather_fusion = bf16[256,32,128]{2,1,0:T(8,128)(2,1)} fusion(bf16[128,32,128]{2,1,0:T(8,128)(2,1)} %all-gather.2.cloned.1.call-done, s32[1024]{0:T(1024)S(1)} %pad_clamp_fusion.1), kind=kCustom, calls=%fused_computation | custom fusion | bytes 4195328 | tf_op jit(solution)/shard_map/jit(_take)/gather | solution.py:17
  54.1 8.5 %fusion.2 = f32[256,32,128]{2,1,0:T(8,128)S(1)} fusion(bf16[1,1,256,128,128]{4,3,2,1,0:T(8,128)(2,1)} %param.5, bf16[256,32,128]{2,1,0:T(8,128)(2,1)} %gather_fusion, pred[256]{0:T(512)(128)(4,1)S(1)} %compare_and_fusion.1), kind=kOutput, calls=%fused_computation.5 | convolution fusion | flops 269484032 | bytes 14680320 | tf_op jit(solution)/shard_map/sef,skf->ske/dot_general | solution.py:18
  62.7 4.5 %fusion.4 = f32[16,32,128]{2,0,1:T(8,128)} fusion(f32[256,32,128]{2,1,0:T(8,128)S(1)} %fusion.2, s32[256]{0:T(256)S(1)} %bitcast.38), kind=kOutput, calls=%fused_computation.7 | convolution fusion | flops 201330688 | bytes 4457472 | tf_op jit(solution)/shard_map/rs,ske->rke/dot_general | solution.py:24
  67.2 0.0 reduce-scatter.3.cloned.1.call-update
  67.2 0.0 reduce-scatter.5.cloned.1.call-start
  67.3 7.7 %fusion = f32[256,32,128]{2,1,0:T(8,128)} fusion(bf16[1,1,256,128,128]{4,3,2,1,0:T(8,128)(2,1)} %param.5, bf16[256,32,128]{2,1,0:T(8,128)(2,1)S(1)} %gather_fusion.1, pred[256]{0:T(512)(128)(4,1)S(1)} %compare_and_fusion), kind=kOutput, calls=%fused_computation.3 | convolution fusion | flops 269484032 | bytes 14680320 | tf_op jit(solution)/shard_map/sef,ske->skf/dot_general | solution.py:27
  74.9 0.2 broadcast_in_dim.23
  75.2 22.6 %scatter_fusion = f32[128,32,128]{2,1,0:T(8,128)S(1)} fusion(f32[128,32,128]{2,1,0:T(8,128)S(1)} %broadcast_in_dim.23, s32[256]{0:T(256)S(1)} %bitcast.36, f32[256,32,128]{2,1,0:T(8,128)} %fusion), kind=kCustom, calls=%fused_computation.2 | custom fusion | flops 1048576 | bytes 12583936 | tf_op jit(solution)/shard_map/scatter-add | solution.py:35
  97.8 0.0 copy-start
  97.8 0.0 copy-start.1
  97.8 0.0 copy-start.2
  97.8 0.0 copy-start.3
  97.9 1.3 copy-done
  99.1 0.0 reduce-scatter.5.cloned.1.call-update
  99.2 0.0 copy-done.1
  99.2 0.3 convolution_bitcast_fusion.1
  99.4 39.7 %psum.7 = f32[32,32]{0,1:T(8,128)S(1)} all-reduce(f32[32,32]{0,1:T(8,128)S(1)} %convolution_bitcast_fusion.1), channel_id=1, replica_groups=mesh['row'=16,'col'=2] {'row','col'}, use_global_device_ids=true, to_apply=%region_1.2 | all-reduce | flops 1024 | bytes 8192 | tf_op jit(solution)/shard_map/psum | solution.py:33
  139.1 0.7 copy.23
  139.8 0.0 copy-done.2
  139.8 0.2 fusion.15
  140.0 0.0 reduce-scatter.3.cloned.1.call-done
  140.0 1.0 bitcast_subtract_fusion
  141.0 0.7 copy.22
  141.7 18.5 %reduce-scatter.5.cloned.1.call-done = f32[8,32,128]{2,1,0:T(8,128)} async-done(((f32[128,32,128]{2,1,0:T(8,128)}), f32[8,32,128]{2,1,0:T(8,128)}) %reduce-scatter.5.cloned.1.call-update) | async-done | bytes 131088 | tf_op jit(solution)/shard_map/reduce_scatter | solution.py:36
  160.2 0.0 copy-done.3
  160.2 1.8 %fusion.10 = f32[8,32,128]{2,1,0:T(8,128)} fusion(f32[8,32,128]{2,1,0:T(8,128)} %reduce-scatter.5.cloned.1.call-done, bf16[8,32,128]{2,1,0:T(8,128)(2,1)S(1)} %copy-done.3, f32[32,32]{0,1:T(8,128)S(1)} %psum.7), kind=kOutput, calls=%fused_computation.14 | convolution fusion | flops 12616704 | bytes 331776 | tf_op jit(solution)/shard_map/tle,kl->tke/dot_general | solution.py:40
  (7 shorter events, 0.0 us)
Async XLA Ops:
  7.2 43.6 %all-gather.2.cloned.1.call-start = ((), (), s32[]{:S(2)}) async-start(), calls=%async_computation.2 | async-start | bytes 1114112 | tf_op jit(solution)/shard_map/all_gather | solution.py:16
  7.9 132.1 %reduce-scatter.3.cloned.1.call-start = ((), (), s32[]{:S(2)}) async-start(), calls=%async_computation.3 | async-start | bytes 393216 | tf_op jit(solution)/shard_map/reduce_scatter | solution.py:34
  14.8 1.0 copy-start.4
  14.8 1.1 copy-start.5
  67.2 93.0 %reduce-scatter.5.cloned.1.call-start = ((), (), s32[]{:S(2)}) async-start(), calls=%async_computation.4 | async-start | bytes 2228224 | tf_op jit(solution)/shard_map/reduce_scatter | solution.py:36
  97.8 1.3 copy-start
  97.8 1.3 copy-start.1
  97.8 42.0 %copy-start.2 = (bf16[8,32,128]{2,1,0:T(8,128)(2,1)S(1)}, bf16[8,32,128]{2,1,0:T(8,128)(2,1)}, u32[]{:S(2)}) copy-start(bf16[8,32,128]{2,1,0:T(8,128)(2,1)} %param.8) | copy-start | bytes 196612
  97.8 62.4 %copy-start.3 = (bf16[8,32,128]{2,1,0:T(8,128)(2,1)S(1)}, bf16[8,32,128]{2,1,0:T(8,128)(2,1)}, u32[]{:S(2)}) copy-start(bf16[8,32,128]{2,1,0:T(8,128)(2,1)} %param.9) | copy-start | bytes 196612
Sparse Core Ops, SparseCore 0:
  10.1 40.5 all-gather.1
  67.3 10.7 reduce-scatter.2
  99.3 60.8 reduce-scatter.4
where the time goes:
time: 169 us
  waiting for transfers between devices  54 us (32%)
  blocking collectives  45.8 us (27%)
  other arithmetic  24.3 us (14%)
  matrix products  23 us (14%)
  between operations  13.9 us (8%)
  local copies, waits for them, and re-layouts  7.34 us (4%)
    psum x1, blocking collectives, per_device(): gram = lax.psum(local_gram, ('row', 'col')) * box_count ** (-0.5)  39.7 us
    all_gather x1, waiting for transfers between devices, per_device(): column_vecs = lax.all_gather(right_vecs, 'row', axis=0, tiled=True)  34.8 us
    scatter-add x1, other arithmetic, per_device(): jax.ops.segment_sum(backward, slot_cols, num_segments=block_cols)  22.6 us
    reduce_scatter x1, waiting for transfers between devices, per_device(): lax.psum_scatter(column_total, 'row', scatter_dimension=0, tiled=True)  18.5 us
    dot_general x1, matrix products, per_device(): jnp.einsum('sef,skf->ske', local_tiles, chosen_right, preferred_element_t...  8.52 us
    dot_general x1, matrix products, per_device(): jnp.einsum('sef,ske->skf', local_tiles, chosen_left, preferred_element_ty...  7.68 us
    all_gather x1, blocking collectives, per_device(): row_vecs = lax.all_gather(left_vecs, 'col', axis=0, tiled=True)  6.17 us
    dot_general x1, matrix products, per_device(): jnp.einsum('rs,ske->rke', row_select, forward, precision=highest)  4.52 us
  transfers between devices with their start and end apart: 3, of which 2 were waited for; matrix products, arithmetic and copies ran while one was open for 21% of the time, Pallas kernels for 0%

commit v1 on v0

v1 whole, which is shorter than its diff:
```python
import functools

import jax
import jax.numpy as jnp
from jax import lax
from jax.experimental import pallas as pl
from jax.experimental.pallas import tpu as pltpu
from jax.sharding import PartitionSpec as P

MESH = pl.DeviceIdType.MESH
F32 = jnp.float32
BF16 = jnp.bfloat16
GROUP = 8


def split(value):
    high = value.astype(BF16)
    low = (value - high.astype(F32)).astype(BF16)
    return high, low


def mul(a, b, dims=(((1,), (0,)), ((), ()))):
    return lax.dot_general(a, b, dims, preferred_element_type=F32)


def kernel(
    sizes,
    row_s,
    col_s,
    row_v,
    col_v,
    right,
    left,
    tiles,
    out_r,
    out_l,
    out_g,
    tbuf,
    cv,
    rv,
    prod,
    zp,
    zc,
    zs,
    zx,
    zz,
    yp,
    yl,
    gz,
    gx,
    gc,
    gy,
    tile_sem,
    send_sem,
    left_sem,
    right_sem,
    zc_sem,
    zx_sem,
    zz_sem,
    y_sem,
    g_sem,
):
    n_r, n_c, outer, inner, chunks = sizes
    piece, vecs, side = right.shape
    slots = tbuf.shape[0]
    step = slots // chunks
    block_rows = piece * n_c
    block_cols = piece * n_r
    part = piece * vecs
    r = lax.axis_index("row")
    c = lax.axis_index("col")
    core = r % 2
    i = (r // 2) % inner
    o = r // (2 * inner)

    def row_of(oo, ii, cc):
        return (oo * inner + ii) * 2 + cc

    partner = (row_of(o, i, 1 - core), c)
    z_far = [(o + d) % outer for d in range(1, outer)]
    z_src = [(o - d + outer) % outer for d in range(1, outer)]
    x_far = [(i + d) % inner for d in range(1, inner)]
    x_src = [(i - d + inner) % inner for d in range(1, inner)]
    y_far = [(c + d) % n_c for d in range(1, n_c)]
    y_src = [(c - d + n_c) % n_c for d in range(1, n_c)]

    def tile_copy(ch):
        at = pl.ds(ch * step, step)
        return pltpu.make_async_copy(tiles.at[0, 0, at], tbuf.at[at], tile_sem.at[ch])

    for ch in range(chunks):
        tile_copy(ch).start()

    barrier = pltpu.get_barrier_semaphore()
    peers = (
        [(row_of(z, i, core), c) for z in z_far]
        + [(row_of(o, x, core), c) for x in x_far]
        + [partner]
        + [(r, y) for y in y_far]
    )
    for peer in peers:
        pl.semaphore_signal(barrier, inc=1, device_id=peer, device_id_type=MESH)
    pl.semaphore_wait(barrier, len(peers))

    sent = []

    def send(src, dst, sem, peer):
        copy = pltpu.make_async_remote_copy(
            src_ref=src,
            dst_ref=dst,
            send_sem=send_sem.at[len(sent)],
            recv_sem=sem,
            device_id=peer,
            device_id_type=MESH,
        )
        copy.start()
        sent.append(copy)

    def landed(ref, sem):
        pltpu.make_async_remote_copy(
            src_ref=ref,
            dst_ref=ref,
            send_sem=send_sem.at[0],
            recv_sem=sem,
            device_id=partner,
            device_id_type=MESH,
        ).wait_recv()

    def cv_at(rr):
        return cv.at[pl.ds(rr * piece, piece)]

    def rv_at(cc):
        return rv.at[pl.ds(cc * piece, piece)]

    for y in y_far:
        send(left, rv_at(c), left_sem.at[c], (r, y))
    for z in z_far:
        send(right, cv_at(r), right_sem.at[r], (row_of(z, i, core), c))
    for x in x_far:
        send(right, cv_at(r), right_sem.at[r], (row_of(o, x, core), c))
    send(right, cv_at(r), right_sem.at[r], partner)
    cv[pl.ds(r * piece, piece)] = right[...]
    rv[pl.ds(c * piece, piece)] = left[...]

    def relay_z():
        for z in z_src:
            got = row_of(z, i, core)
            landed(cv_at(got), right_sem.at[got])
            for x in x_far:
                send(cv_at(got), cv_at(got), right_sem.at[got], (row_of(o, x, core), c))
            send(cv_at(got), cv_at(got), right_sem.at[got], partner)

    def relay_x():
        for z in [o] + z_src:
            for x in x_src:
                got = row_of(z, x, core)
                landed(cv_at(got), right_sem.at[got])
                send(cv_at(got), cv_at(got), right_sem.at[got], partner)

    def take_core():
        for z in [o] + z_src:
            for x in [i] + x_src:
                got = row_of(z, x, 1 - core)
                landed(cv_at(got), right_sem.at[got])

    def images(ch, vec_ref, index, limit, dims):
        def body(g, carry):
            for u in range(GROUP):
                s = ch * step + g * GROUP + u
                x = vec_ref[jnp.minimum(index[s], limit - 1)]
                prod[pl.ds(pl.multiple_of(s * vecs, vecs), vecs), :] = mul(x, tbuf[s], dims)
            return carry

        lax.fori_loop(0, step // GROUP, body, 0)

    plain = (((1,), (0,)), ((), ()))
    across = (((1,), (1,)), ((), ()))

    def gather_sums(index_v, rows, target):
        pick = lax.broadcasted_iota(jnp.int32, (rows, slots), 0) == index_v[...]
        pick = jnp.where(pick, 1.0, 0.0).astype(BF16)

        def body(k, carry):
            high, low = split(prod[pl.ds(k, slots, stride=vecs), :])
            target[pl.ds(k, rows, stride=vecs), :] = mul(pick, high) + mul(pick, low)
            return carry

        lax.fori_loop(0, vecs, body, 0)

    for y in y_src:
        landed(rv_at(y), left_sem.at[y])
    for ch in range(chunks):
        tile_copy(ch).wait()
        images(ch, rv, row_s, block_rows, plain)
        if ch == chunks // 2:
            relay_z()
    relay_x()
    gather_sums(col_v, block_cols, zp)

    z_order = list(zip(z_far, range(1, outer))) + [(o, 0)]
    x_order = list(zip(x_far, range(1, inner))) + [(i, 0)]
    for z, _ in z_order:
        for x, _ in x_order:
            at = pl.ds(row_of(z, x, 1 - core) * part, part)
            slot = z * inner + x
            send(zp.at[at], zc.at[slot], zc_sem.at[slot], partner)
    take_core()
    for ch in range(chunks // 2):
        images(ch, cv, col_s, block_cols, across)
    for z, _ in z_order:
        for x, dx in x_order:
            slot = z * inner + x
            landed(zc.at[slot], zc_sem.at[slot])
            at = pl.ds(row_of(z, x, core) * part, part)
            zs[slot] = zp[at] + zc[slot]
            if dx:
                send(zs.at[slot], zx.at[dx - 1, z], zx_sem.at[dx - 1, z], (row_of(o, x, core), c))
    for ch in range(chunks // 2, chunks):
        images(ch, cv, col_s, block_cols, across)
    gather_sums(row_v, block_rows, yp)
    for y in y_far:
        dy = (y - c + n_c) % n_c
        send(yp.at[pl.ds(y * part, part)], yl.at[dy], y_sem.at[dy], (r, y))

    def gram_step(a, total):
        at = pl.ds(pl.multiple_of(a * vecs, vecs), vecs)
        high, low = split(yp[at, :])
        mine = rv[a]
        return total + mul(mine, high, across) + mul(mine, low, across)

    gram = lax.fori_loop(0, block_rows, gram_step, jnp.zeros((vecs, vecs), F32))
    used = 0

    def spread(value, buf, me, far, src, peer):
        nonlocal used
        buf[me] = value
        for f in far:
            send(buf.at[me], buf.at[me], g_sem.at[used + me], peer(f))
        for s in src:
            landed(buf.at[s], g_sem.at[used + s])
        used += buf.shape[0]
        total = buf[0]
        for q in range(1, buf.shape[0]):
            total = total + buf[q]
        return total

    gram = spread(gram, gc, core, [1 - core], [1 - core], lambda f: (row_of(o, i, f), c))
    gram = spread(gram, gx, i, x_far, x_src, lambda f: (row_of(o, f, core), c))

    for z, dz in z_order:
        slot = z * inner + i
        total = zs[slot]
        for d in range(1, inner):
            landed(zx.at[d - 1, z], zx_sem.at[d - 1, z])
            total = total + zx[d - 1, z]
        zs[slot] = total
        if dz:
            send(zs.at[slot], zz.at[dz - 1], zz_sem.at[dz - 1], (row_of(z, i, core), c))

    gram = spread(gram, gy, c, y_far, y_src, lambda f: (r, f))
    gram = spread(gram, gz, o, z_far, z_src, lambda f: (row_of(f, i, core), c))
    gram = gram * (block_cols * n_c * side) ** (-0.5)
    out_g[...] = gram
    high, low = split(gram)
    turned = gram.T
    turned_high, turned_low = split(turned)

    y_total = yp[pl.ds(c * part, part), :]
    for d in range(1, n_c):
        landed(yl.at[d], y_sem.at[d])
        y_total = y_total + yl[d]
    for t in range(piece):
        at = slice(t * vecs, (t + 1) * vecs)
        out_r[t] = y_total[at] - (mul(turned_high, right[t]) + mul(turned_low, right[t]))
    z_total = zs[o * inner + i]
    for d in range(1, outer):
        landed(zz.at[d - 1], zz_sem.at[d - 1])
        z_total = z_total + zz[d - 1]
    for t in range(piece):
        at = slice(t * vecs, (t + 1) * vecs)
        out_l[t] = z_total[at] - (mul(high, left[t]) + mul(low, left[t]))
    for copy in sent:
        copy.wait_send()


def solution(mesh):
    n_r, n_c = mesh.shape["row"], mesh.shape["col"]
    half = n_r // 2
    inner = 1 << ((half.bit_length() - 1) // 2)
    outer = half // inner

    def per_device(tiles, tile_row, tile_col, right_vecs, left_vecs):
        slots, side = tiles.shape[2], tiles.shape[3]
        piece, vecs, _ = right_vecs.shape
        chunks = 8
        part = piece * vecs
        block_rows, block_cols = piece * n_c, piece * n_r
        planes = outer * inner
        sends = (
            2 * (n_c - 1)
            + (outer - 1)
            + (inner - 1)
            + 1
            + (outer - 1) * inner
            + outer * (inner - 1)
            + planes
            + outer * (inner - 1)
            + (outer - 1)
            + 1
            + (inner - 1)
            + (n_c - 1)
            + (outer - 1)
        )
        vmem = pl.BlockSpec(memory_space=pltpu.VMEM)
        smem = pl.BlockSpec(memory_space=pltpu.SMEM)
        dma = pltpu.SemaphoreType.DMA
        row_s = tile_row.reshape(slots)
        col_s = tile_col.reshape(slots)
        return pl.pallas_call(
            functools.partial(kernel, (n_r, n_c, outer, inner, chunks)),
            out_shape=(
                jax.ShapeDtypeStruct((piece, vecs, side), F32),
                jax.ShapeDtypeStruct((piece, vecs, side), F32),
                jax.ShapeDtypeStruct((vecs, vecs), F32),
            ),
            in_specs=[smem, smem, vmem, vmem, vmem, vmem, pl.BlockSpec(memory_space=pl.ANY)],
            out_specs=(vmem, vmem, vmem),
            scratch_shapes=[
                pltpu.VMEM((slots, side, side), BF16),
                pltpu.VMEM((block_cols, vecs, side), BF16),
                pltpu.VMEM((block_rows, vecs, side), BF16),
                pltpu.VMEM((slots * vecs, side), F32),
                pltpu.VMEM((block_cols * vecs, side), F32),
                pltpu.VMEM((planes, part, side), F32),
                pltpu.VMEM((planes, part, side), F32),
                pltpu.VMEM((max(inner - 1, 1), outer, part, side), F32),
                pltpu.VMEM((max(outer - 1, 1), part, side), F32),
                pltpu.VMEM((block_rows * vecs, side), F32),
                pltpu.VMEM((n_c, part, side), F32),
                pltpu.VMEM((outer, vecs, vecs), F32),
                pltpu.VMEM((inner, vecs, vecs), F32),
                pltpu.VMEM((2, vecs, vecs), F32),
                pltpu.VMEM((n_c, vecs, vecs), F32),
                dma((chunks,)),
                dma((sends,)),
                dma((n_c,)),
                dma((n_r,)),
                dma((planes,)),
                dma((max(inner - 1, 1), outer)),
                dma((max(outer - 1, 1),)),
                dma((n_c,)),
                dma((outer + inner + 2 + n_c,)),
            ],
            compiler_params=pltpu.CompilerParams(
                collective_id=0, has_side_effects=True, vmem_limit_bytes=60 * 1024 * 1024
            ),
            name="arnoldi_step",
        )(row_s, col_s, row_s.reshape(1, slots), col_s.reshape(1, slots), right_vecs, left_vecs, tiles)

    placed = (
        P("row", "col", None, None, None),
        P("row", "col", None),
        P("row", "col", None),
        P(("row", "col"), None, None),
        P(("row", "col"), None, None),
    )
    return jax.shard_map(
        per_device,
        mesh=mesh,
        in_specs=placed,
        out_specs=(P(("row", "col"), None, None), P(("row", "col"), None, None), P()),
        check_vma=False,
    )
```

time: 169 us -> 72.1 us (0.43)
  Pallas kernels: 0 us -> 66.7 us
  waiting for transfers between devices: 54 us -> 0 us
  blocking collectives: 45.8 us -> 0 us
  other arithmetic: 24.3 us -> 0 us
  matrix products: 23 us -> 0 us
  between operations: 13.9 us -> 0.64 us
  local copies, waits for them, and re-layouts: 7.34 us -> 4.46 us
    pallas_call x0 -> x1, Pallas kernels: none -> 66.7 us  [per_device(): pl.pallas_call(functools.partial(kernel, (n_r, n_c, outer, inner, chunks)...]
    psum x1 -> x0, blocking collectives: 39.7 us -> none  [per_device(): gram = lax.psum(local_gram, ('row', 'col')) * box_count ** (-0.5)]
    all_gather x1 -> x0, waiting for transfers between devices: 34.8 us -> none  [per_device(): column_vecs = lax.all_gather(right_vecs, 'row', axis=0, tiled=True)]
    dot_general x6 -> x0, matrix products: 23 us -> none  [the longest x1 8.52 us: per_device(): jnp.einsum('sef,skf->ske', local_tiles, chosen_right, preferred_element_t...]
    scatter-add x1 -> x0, other arithmetic: 22.6 us -> none  [per_device(): jax.ops.segment_sum(backward, slot_cols, num_segments=block_cols)]
    reduce_scatter x2 -> x0, waiting for transfers between devices: 18.5 us -> none  [the longest x1 18.5 us: per_device(): lax.psum_scatter(column_total, 'row', scatter_dimension=0, tiled=True)]
    all_gather x1 -> x0, blocking collectives: 6.17 us -> none  [per_device(): row_vecs = lax.all_gather(left_vecs, 'col', axis=0, tiled=True)]
    gather x2 -> x0, local copies, waits for them, and re-layouts: 4.41 us -> none  [the longest x1 3.41 us: per_device(): jnp.take(column_vecs, jnp.minimum(slot_cols, block_cols - 1), axis=0)]
  transfers between devices with their start and end apart: 3 -> 0, of which waited for: 2 -> 0; matrix products, arithmetic and copies ran while one was open for 21% -> 0% of each run, Pallas kernels for 0% -> 0%
where the time goes in v1:
time: 72.1 us; the launch traced here: 71.8 us
  Pallas kernels  66.7 us (93%)
  local copies, waits for them, and re-layouts  4.46 us (6%)
    pallas_call x1, Pallas kernels, per_device(): pl.pallas_call(functools.partial(kernel, (n_r, n_c, outer, inner, chunks)...  66.7 us
    unnamed x3, local copies, waits for them, and re-layouts  4.46 us

profile of v1, /device:TPU:0, one launch (start us, length us, event | category | flops | bytes accessed | tf_op | source)
XLA Modules:
  0.0 71.8 jit_solution(16235767018826086582)
XLA Ops:
  0.6 66.7 %arnoldi_step.1 = (f32[8,32,128]{2,1,0:T(8,128)}, f32[8,32,128]{2,1,0:T(8,128)}, f32[32,32]{1,0:T(8,128)}) custom-call(s32[256]{0:T(256)} %bitcast.4, s32[256]{0:T(256)} %bitcast.6, s32[1,256]{1,0:T(1,128)} %bitcast.5, s32[1,256]{1,0:T(1,128)} %bitcast.7, bf16[8,32,128]{2,1,0:T(8,128)(2,1)} %right.1, bf16[8,32,128]{2,1,0:T(8,128)(2,1)} %left.1, ...), custom_call_target="tpu_custom_call" | custom-call | tf_op jit(solution)/shard_map/arnoldi_step/pallas_call | solution.py:319
  67.4 1.6 %copy.11 = f32[8,32,128]{2,1,0:T(8,128)} copy(f32[8,32,128]{2,1,0:T(8,128)} %get-tuple-element.6) | data formatting | bytes 262144
  68.9 1.6 %copy.12 = f32[8,32,128]{2,1,0:T(8,128)} copy(f32[8,32,128]{2,1,0:T(8,128)} %get-tuple-element.7) | data formatting | bytes 262144
  70.5 1.3 %copy.13 = f32[32,32]{1,0:T(8,128)} copy(f32[32,32]{1,0:T(8,128)} %get-tuple-element.8) | data formatting | bytes 8192

commit v2 on v1

--- a/solution.py
+++ b/solution.py
@@ -11,6 +11,7 @@
 F32 = jnp.float32
 BF16 = jnp.bfloat16
 GROUP = 8
+PAD = 1
 
 
 def split(value):
@@ -32,8 +33,8 @@
     right,
     left,
     tiles,
-    out_r,
-    out_l,
+    out_y,
+    out_z,
     out_g,
     tbuf,
     cv,
@@ -66,7 +67,8 @@
     step = slots // chunks
     block_rows = piece * n_c
     block_cols = piece * n_r
-    part = piece * vecs
+    wide = vecs + PAD
+    part = piece * wide
     r = lax.axis_index("row")
     c = lax.axis_index("col")
     core = r % 2
@@ -168,7 +170,7 @@
             for u in range(GROUP):
                 s = ch * step + g * GROUP + u
                 x = vec_ref[jnp.minimum(index[s], limit - 1)]
-                prod[pl.ds(pl.multiple_of(s * vecs, vecs), vecs), :] = mul(x, tbuf[s], dims)
+                prod[pl.ds(s * wide, vecs), :] = mul(x, tbuf[s], dims)
             return carry
 
         lax.fori_loop(0, step // GROUP, body, 0)
@@ -181,8 +183,8 @@
         pick = jnp.where(pick, 1.0, 0.0).astype(BF16)
 
         def body(k, carry):
-            high, low = split(prod[pl.ds(k, slots, stride=vecs), :])
-            target[pl.ds(k, rows, stride=vecs), :] = mul(pick, high) + mul(pick, low)
+            high, low = split(prod[pl.ds(k, slots, stride=wide), :])
+            target[pl.ds(k, rows, stride=wide), :] = mul(pick, high) + mul(pick, low)
             return carry
 
         lax.fori_loop(0, vecs, body, 0)
@@ -223,7 +225,7 @@
         send(yp.at[pl.ds(y * part, part)], yl.at[dy], y_sem.at[dy], (r, y))
 
     def gram_step(a, total):
-        at = pl.ds(pl.multiple_of(a * vecs, vecs), vecs)
+        at = pl.ds(a * wide, vecs)
         high, low = split(yp[at, :])
         mine = rv[a]
         return total + mul(mine, high, across) + mul(mine, low, across)
@@ -261,26 +263,31 @@
     gram = spread(gram, gz, o, z_far, z_src, lambda f: (row_of(f, i, core), c))
     gram = gram * (block_cols * n_c * side) ** (-0.5)
     out_g[...] = gram
-    high, low = split(gram)
-    turned = gram.T
-    turned_high, turned_low = split(turned)
-
     y_total = yp[pl.ds(c * part, part), :]
     for d in range(1, n_c):
         landed(yl.at[d], y_sem.at[d])
         y_total = y_total + yl[d]
-    for t in range(piece):
-        at = slice(t * vecs, (t + 1) * vecs)
-        out_r[t] = y_total[at] - (mul(turned_high, right[t]) + mul(turned_low, right[t]))
+    out_y[...] = y_total
     z_total = zs[o * inner + i]
     for d in range(1, outer):
         landed(zz.at[d - 1], zz_sem.at[d - 1])
         z_total = z_total + zz[d - 1]
-    for t in range(piece):
-        at = slice(t * vecs, (t + 1) * vecs)
-        out_l[t] = z_total[at] - (mul(high, left[t]) + mul(low, left[t]))
+    out_z[...] = z_total
     for copy in sent:
         copy.wait_send()
+
+
+def finish(y_ref, z_ref, gram_ref, right, left, out_r, out_l, out_g):
+    piece, vecs, _ = right.shape
+    wide = y_ref.shape[0] // piece
+    gram = gram_ref[...]
+    out_g[...] = gram
+    high, low = split(gram)
+    turned_high, turned_low = split(gram.T)
+    for t in range(piece):
+        at = slice(t * wide, t * wide + vecs)
+        out_r[t] = y_ref[at] - (mul(turned_high, right[t]) + mul(turned_low, right[t]))
+        out_l[t] = z_ref[at] - (mul(high, left[t]) + mul(low, left[t]))
 
 
 def solution(mesh):
@@ -293,7 +300,8 @@
         slots, side = tiles.shape[2], tiles.shape[3]
         piece, vecs, _ = right_vecs.shape
         chunks = 8
-        part = piece * vecs
+        wide = vecs + PAD
+        part = piece * wide
         block_rows, block_cols = piece * n_c, piece * n_r
         planes = outer * inner
         sends = (
@@ -316,11 +324,11 @@
         dma = pltpu.SemaphoreType.DMA
         row_s = tile_row.reshape(slots)
         col_s = tile_col.reshape(slots)
-        return pl.pallas_call(
+        y_total, z_total, gram = pl.pallas_call(
             functools.partial(kernel, (n_r, n_c, outer, inner, chunks)),
             out_shape=(
-                jax.ShapeDtypeStruct((piece, vecs, side), F32),
-                jax.ShapeDtypeStruct((piece, vecs, side), F32),
+                jax.ShapeDtypeStruct((part, side), F32),
+                jax.ShapeDtypeStruct((part, side), F32),
                 jax.ShapeDtypeStruct((vecs, vecs), F32),
             ),
             in_specs=[smem, smem, vmem, vmem, vmem, vmem, pl.BlockSpec(memory_space=pl.ANY)],
@@ -329,13 +337,13 @@
                 pltpu.VMEM((slots, side, side), BF16),
                 pltpu.VMEM((block_cols, vecs, side), BF16),
                 pltpu.VMEM((block_rows, vecs, side), BF16),
-                pltpu.VMEM((slots * vecs, side), F32),
-                pltpu.VMEM((block_cols * vecs, side), F32),
+                pltpu.VMEM((slots * wide, side), F32),
+                pltpu.VMEM((block_cols * wide, side), F32),
                 pltpu.VMEM((planes, part, side), F32),
                 pltpu.VMEM((planes, part, side), F32),
                 pltpu.VMEM((max(inner - 1, 1), outer, part, side), F32),
                 pltpu.VMEM((max(outer - 1, 1), part, side), F32),
-                pltpu.VMEM((block_rows * vecs, side), F32),
+                pltpu.VMEM((block_rows * wide, side), F32),
                 pltpu.VMEM((n_c, part, side), F32),
                 pltpu.VMEM((outer, vecs, vecs), F32),
                 pltpu.VMEM((inner, vecs, vecs), F32),
@@ -356,6 +364,17 @@
             ),
             name="arnoldi_step",
         )(row_s, col_s, row_s.reshape(1, slots), col_s.reshape(1, slots), right_vecs, left_vecs, tiles)
+        return pl.pallas_call(
+            finish,
+            out_shape=(
+                jax.ShapeDtypeStruct((piece, vecs, side), F32),
+                jax.ShapeDtypeStruct((piece, vecs, side), F32),
+                jax.ShapeDtypeStruct((vecs, vecs), F32),
+            ),
+            in_specs=[vmem] * 5,
+            out_specs=(vmem, vmem, vmem),
+            name="finish",
+        )(y_total, z_total, gram, right_vecs, left_vecs)
 
     placed = (
         P("row", "col", None, None, None),

time: 72.1 us -> 60.7 us (0.84)
  Pallas kernels: 66.7 us -> 59.9 us
  local copies, waits for them, and re-layouts: 4.46 us -> 0 us
    pallas_call x1, Pallas kernels: 66.7 us -> 57.9 us  [per_device(): pl.pallas_call(functools.partial(kernel, (n_r, n_c, outer, inner, chunks)...]
    unnamed x3 -> x0, local copies, waits for them, and re-layouts: 4.46 us -> none
    pallas_call x0 -> x1, Pallas kernels: none -> 1.96 us  [per_device(): pl.pallas_call(finish, out_shape=(jax.ShapeDtypeStruct((piece, vecs, side...]
where the time goes in v2:
time: 60.7 us; the launch traced here: 60.5 us
  Pallas kernels  59.9 us (99%)
  between operations  0.64 us (1%)
    pallas_call x1, Pallas kernels, per_device(): pl.pallas_call(functools.partial(kernel, (n_r, n_c, outer, inner, chunks)...  57.9 us
    pallas_call x1, Pallas kernels, per_device(): pl.pallas_call(finish, out_shape=(jax.ShapeDtypeStruct((piece, vecs, side...  1.96 us

profile of v2, /device:TPU:0, one launch (start us, length us, event | category | flops | bytes accessed | tf_op | source)
XLA Modules:
  0.0 60.5 jit_solution(4771451539155298163)
XLA Ops:
  0.6 57.9 %arnoldi_step.1 = (f32[264,128]{1,0:T(8,128)}, f32[264,128]{1,0:T(8,128)}, f32[32,32]{1,0:T(8,128)}) custom-call(s32[256]{0:T(256)} %bitcast.4, s32[256]{0:T(256)} %bitcast.6, s32[1,256]{1,0:T(1,128)} %bitcast.5, s32[1,256]{1,0:T(1,128)} %bitcast.7, bf16[8,32,128]{2,1,0:T(8,128)(2,1)} %right.3, bf16[8,32,128]{2,1,0:T(8,128)(2,1)} %left.3, ...), custom_call_target="tpu_custom_call" | custom-call | tf_op jit(solution)/shard_map/arnoldi_step/pallas_call | solution.py:327
  58.6 2.0 %finish.1 = (f32[8,32,128]{2,1,0:T(8,128)}, f32[8,32,128]{2,1,0:T(8,128)}, f32[32,32]{1,0:T(8,128)}) custom-call(f32[264,128]{1,0:T(8,128)} %get-tuple-element.6.y_ref, f32[264,128]{1,0:T(8,128)} %get-tuple-element.7.z_ref, f32[32,32]{1,0:T(8,128)} %get-tuple-element.8.gram_ref, bf16[8,32,128]{2,1,0:T(8,128)(2,1)} %right.3, bf16[8,32,128]{2,1,0:T(8,128)(2,1)} %left.3), custom_call_target="tpu_custom_call" | custom-call | tf_op jit(solution)/shard_map/finish/pallas_call | solution.py:367

commit v3 on v2

--- a/solution.py
+++ b/solution.py
@@ -10,7 +10,11 @@
 MESH = pl.DeviceIdType.MESH
 F32 = jnp.float32
 BF16 = jnp.bfloat16
-GROUP = 8
+GROUP = 32
+PAIR = 2
+KGROUP = 8
+TOP = 32767.0
+LEAST = 2.0**-110
 PAD = 1
 
 
@@ -43,8 +47,14 @@
     zp,
     zc,
     zs,
-    zx,
-    zz,
+    qx_out,
+    sx_out,
+    qx,
+    sx,
+    qz_out,
+    sz_out,
+    qz,
+    sz,
     yp,
     yl,
     gz,
@@ -58,6 +68,8 @@
     zc_sem,
     zx_sem,
     zz_sem,
+    sx_sem,
+    sz_sem,
     y_sem,
     g_sem,
 ):
@@ -165,12 +177,17 @@
                 got = row_of(z, x, 1 - core)
                 landed(cv_at(got), right_sem.at[got])
 
-    def images(ch, vec_ref, index, limit, dims):
+    def images(ch, vec_ref, index, limit, turned):
         def body(g, carry):
-            for u in range(GROUP):
+            for u in range(0, GROUP, PAIR):
                 s = ch * step + g * GROUP + u
-                x = vec_ref[jnp.minimum(index[s], limit - 1)]
-                prod[pl.ds(s * wide, vecs), :] = mul(x, tbuf[s], dims)
+                xs = [vec_ref[jnp.minimum(index[s + q], limit - 1)] for q in range(PAIR)]
+                ts = [tbuf[s + q] for q in range(PAIR)]
+                dims = across if turned else plain
+                got = mul(jnp.concatenate(xs, 0), jnp.concatenate(ts, 0 if turned else 1), dims)
+                for q in range(PAIR):
+                    block = got[q * vecs : (q + 1) * vecs, q * side : (q + 1) * side]
+                    prod[pl.ds((s + q) * wide, vecs), :] = block
             return carry
 
         lax.fori_loop(0, step // GROUP, body, 0)
@@ -181,22 +198,28 @@
     def gather_sums(index_v, rows, target):
         pick = lax.broadcasted_iota(jnp.int32, (rows, slots), 0) == index_v[...]
         pick = jnp.where(pick, 1.0, 0.0).astype(BF16)
-
-        def body(k, carry):
-            high, low = split(prod[pl.ds(k, slots, stride=wide), :])
-            target[pl.ds(k, rows, stride=wide), :] = mul(pick, high) + mul(pick, low)
+        pick = jnp.concatenate([pick, pick], 1)
+
+        def body(g, carry):
+            for u in range(0, KGROUP, PAIR):
+                k = g * KGROUP + u
+                terms = [split(prod[pl.ds(k + q, slots, stride=wide), :]) for q in range(PAIR)]
+                high = jnp.concatenate([t[0] for t in terms], 1)
+                low = jnp.concatenate([t[1] for t in terms], 1)
+                got = mul(pick, jnp.concatenate([high, low], 0))
+                for q in range(PAIR):
+                    block = got[:, q * side : (q + 1) * side]
+                    target[pl.ds(k + q, rows, stride=wide), :] = block
             return carry
 
-        lax.fori_loop(0, vecs, body, 0)
+        lax.fori_loop(0, vecs // KGROUP, body, 0)
 
     for y in y_src:
         landed(rv_at(y), left_sem.at[y])
     for ch in range(chunks):
         tile_copy(ch).wait()
-        images(ch, rv, row_s, block_rows, plain)
-        if ch == chunks // 2:
-            relay_z()
-    relay_x()
+        images(ch, rv, row_s, block_rows, False)
+    relay_z()
     gather_sums(col_v, block_cols, zp)
 
     z_order = list(zip(z_far, range(1, outer))) + [(o, 0)]
@@ -206,19 +229,40 @@
             at = pl.ds(row_of(z, x, 1 - core) * part, part)
             slot = z * inner + x
             send(zp.at[at], zc.at[slot], zc_sem.at[slot], partner)
+    relay_x()
     take_core()
     for ch in range(chunks // 2):
-        images(ch, cv, col_s, block_cols, across)
+        images(ch, cv, col_s, block_cols, True)
+    def encode(block_of, q_ref, s_ref):
+        scales = []
+        for t in range(piece):
+            block = block_of(t)
+            top = jnp.maximum(jnp.max(jnp.abs(block), axis=0, keepdims=True), LEAST)
+            q_ref[t * vecs : (t + 1) * vecs] = (
+                jnp.round(block * (TOP / top)).astype(jnp.int32).astype(jnp.int16)
+            )
+            scales.append(top * (1.0 / TOP))
+        s_ref[...] = jnp.concatenate(scales, 0)
+
+    def decode(q_ref, s_ref, t):
+        code = q_ref[t * vecs : (t + 1) * vecs].astype(jnp.int32).astype(F32)
+        return code * s_ref[t : t + 1]
+
+    def pair_sum(z, x, t):
+        mine = zp[pl.ds(row_of(z, x, core) * part + t * wide, vecs), :]
+        return mine + zc[z * inner + x, t * wide : t * wide + vecs]
+
     for z, _ in z_order:
         for x, dx in x_order:
             slot = z * inner + x
             landed(zc.at[slot], zc_sem.at[slot])
-            at = pl.ds(row_of(z, x, core) * part, part)
-            zs[slot] = zp[at] + zc[slot]
             if dx:
-                send(zs.at[slot], zx.at[dx - 1, z], zx_sem.at[dx - 1, z], (row_of(o, x, core), c))
+                encode(functools.partial(pair_sum, z, x), qx_out.at[dx - 1, z], sx_out.at[dx - 1, z])
+                peer = (row_of(o, x, core), c)
+                send(qx_out.at[dx - 1, z], qx.at[dx - 1, z], zx_sem.at[dx - 1, z], peer)
+                send(sx_out.at[dx - 1, z], sx.at[dx - 1, z], sx_sem.at[dx - 1, z], peer)
     for ch in range(chunks // 2, chunks):
-        images(ch, cv, col_s, block_cols, across)
+        images(ch, cv, col_s, block_cols, True)
     gather_sums(row_v, block_rows, yp)
     for y in y_far:
         dy = (y - c + n_c) % n_c
@@ -249,15 +293,24 @@
     gram = spread(gram, gc, core, [1 - core], [1 - core], lambda f: (row_of(o, i, f), c))
     gram = spread(gram, gx, i, x_far, x_src, lambda f: (row_of(o, f, core), c))
 
+    def plane_sum(z, t):
+        total = pair_sum(z, i, t)
+        for d in range(1, inner):
+            total = total + decode(qx.at[d - 1, z], sx.at[d - 1, z], t)
+        return total
+
     for z, dz in z_order:
-        slot = z * inner + i
-        total = zs[slot]
         for d in range(1, inner):
-            landed(zx.at[d - 1, z], zx_sem.at[d - 1, z])
-            total = total + zx[d - 1, z]
-        zs[slot] = total
+            landed(qx.at[d - 1, z], zx_sem.at[d - 1, z])
+            landed(sx.at[d - 1, z], sx_sem.at[d - 1, z])
         if dz:
-            send(zs.at[slot], zz.at[dz - 1], zz_sem.at[dz - 1], (row_of(z, i, core), c))
+            encode(functools.partial(plane_sum, z), qz_out.at[dz - 1], sz_out.at[dz - 1])
+            peer = (row_of(z, i, core), c)
+            send(qz_out.at[dz - 1], qz.at[dz - 1], zz_sem.at[dz - 1], peer)
+            send(sz_out.at[dz - 1], sz.at[dz - 1], sz_sem.at[dz - 1], peer)
+        else:
+            for t in range(piece):
+                zs[t * vecs : (t + 1) * vecs] = plane_sum(z, t)
 
     gram = spread(gram, gy, c, y_far, y_src, lambda f: (r, f))
     gram = spread(gram, gz, o, z_far, z_src, lambda f: (row_of(f, i, core), c))
@@ -268,11 +321,14 @@
         landed(yl.at[d], y_sem.at[d])
         y_total = y_total + yl[d]
     out_y[...] = y_total
-    z_total = zs[o * inner + i]
     for d in range(1, outer):
-        landed(zz.at[d - 1], zz_sem.at[d - 1])
-        z_total = z_total + zz[d - 1]
-    out_z[...] = z_total
+        landed(qz.at[d - 1], zz_sem.at[d - 1])
+        landed(sz.at[d - 1], sz_sem.at[d - 1])
+    for t in range(piece):
+        total = zs[t * vecs : (t + 1) * vecs]
+        for d in range(1, outer):
+            total = total + decode(qz.at[d - 1], sz.at[d - 1], t)
+        out_z[t] = total
     for copy in sent:
         copy.wait_send()
 
@@ -287,7 +343,7 @@
     for t in range(piece):
         at = slice(t * wide, t * wide + vecs)
         out_r[t] = y_ref[at] - (mul(turned_high, right[t]) + mul(turned_low, right[t]))
-        out_l[t] = z_ref[at] - (mul(high, left[t]) + mul(low, left[t]))
+        out_l[t] = z_ref[t] - (mul(high, left[t]) + mul(low, left[t]))
 
 
 def solution(mesh):
@@ -304,6 +360,7 @@
         part = piece * wide
         block_rows, block_cols = piece * n_c, piece * n_r
         planes = outer * inner
+        near, far = max(inner - 1, 1), max(outer - 1, 1)
         sends = (
             2 * (n_c - 1)
             + (outer - 1)
@@ -312,8 +369,8 @@
             + (outer - 1) * inner
             + outer * (inner - 1)
             + planes
-            + outer * (inner - 1)
-            + (outer - 1)
+            + 2 * outer * (inner - 1)
+            + 2 * (outer - 1)
             + 1
             + (inner - 1)
             + (n_c - 1)
@@ -328,7 +385,7 @@
             functools.partial(kernel, (n_r, n_c, outer, inner, chunks)),
             out_shape=(
                 jax.ShapeDtypeStruct((part, side), F32),
-                jax.ShapeDtypeStruct((part, side), F32),
+                jax.ShapeDtypeStruct((piece, vecs, side), F32),
                 jax.ShapeDtypeStruct((vecs, vecs), F32),
             ),
             in_specs=[smem, smem, vmem, vmem, vmem, vmem, pl.BlockSpec(memory_space=pl.ANY)],
@@ -340,9 +397,12 @@
                 pltpu.VMEM((slots * wide, side), F32),
                 pltpu.VMEM((block_cols * wide, side), F32),
                 pltpu.VMEM((planes, part, side), F32),
-                pltpu.VMEM((planes, part, side), F32),
-                pltpu.VMEM((max(inner - 1, 1), outer, part, side), F32),
-                pltpu.VMEM((max(outer - 1, 1), part, side), F32),
+                pltpu.VMEM((piece * vecs, side), F32),
+                *[
+                    pltpu.VMEM(lead + shape, kind)
+                    for lead in [(near, outer)] * 2 + [(far,)] * 2
+                    for shape, kind in [((piece * vecs, side), jnp.int16), ((piece, side), F32)]
+                ],
                 pltpu.VMEM((block_rows * wide, side), F32),
                 pltpu.VMEM((n_c, part, side), F32),
                 pltpu.VMEM((outer, vecs, vecs), F32),
@@ -354,8 +414,7 @@
                 dma((n_c,)),
                 dma((n_r,)),
                 dma((planes,)),
-                dma((max(inner - 1, 1), outer)),
-                dma((max(outer - 1, 1),)),
+                *[dma((near, outer)), dma((far,))] * 2,
                 dma((n_c,)),
                 dma((outer + inner + 2 + n_c,)),
             ],

time: 60.7 us -> 40.6 us (0.67)
  Pallas kernels: 59.9 us -> 39.8 us
    pallas_call x1, Pallas kernels: 57.9 us -> 37.9 us  [per_device(): pl.pallas_call(functools.partial(kernel, (n_r, n_c, outer, inner, chunks)...]
where the time goes in v3:
time: 40.6 us; the launch traced here: 40.5 us
  Pallas kernels  39.8 us (98%)
  between operations  0.64 us (2%)
    pallas_call x1, Pallas kernels, per_device(): pl.pallas_call(functools.partial(kernel, (n_r, n_c, outer, inner, chunks)...  37.9 us
    pallas_call x1, Pallas kernels, per_device(): pl.pallas_call(finish, out_shape=(jax.ShapeDtypeStruct((piece, vecs, side...  1.95 us

profile of v3, /device:TPU:0, one launch (start us, length us, event | category | flops | bytes accessed | tf_op | source)
XLA Modules:
  0.0 40.5 jit_solution(5917333707205173862)
XLA Ops:
  0.6 37.9 %arnoldi_step.1 = (f32[264,128]{1,0:T(8,128)}, f32[8,32,128]{2,1,0:T(8,128)}, f32[32,32]{1,0:T(8,128)}) custom-call(s32[256]{0:T(256)} %bitcast.4, s32[256]{0:T(256)} %bitcast.6, s32[1,256]{1,0:T(1,128)} %bitcast.5, s32[1,256]{1,0:T(1,128)} %bitcast.7, bf16[8,32,128]{2,1,0:T(8,128)(2,1)} %right.3, bf16[8,32,128]{2,1,0:T(8,128)(2,1)} %left.3, ...), custom_call_target="tpu_custom_call" | custom-call | tf_op jit(solution)/shard_map/arnoldi_step/pallas_call | solution.py:384
  38.5 2.0 %finish.1 = (f32[8,32,128]{2,1,0:T(8,128)}, f32[8,32,128]{2,1,0:T(8,128)}, f32[32,32]{1,0:T(8,128)}) custom-call(f32[264,128]{1,0:T(8,128)} %get-tuple-element.6.y_ref, f32[8,32,128]{2,1,0:T(8,128)} %get-tuple-element.7.z_ref, f32[32,32]{1,0:T(8,128)} %get-tuple-element.8.gram_ref, bf16[8,32,128]{2,1,0:T(8,128)(2,1)} %right.3, bf16[8,32,128]{2,1,0:T(8,128)(2,1)} %left.3), custom_call_target="tpu_custom_call" | custom-call | tf_op jit(solution)/shard_map/finish/pallas_call | solution.py:426

commit v4 on v3

--- a/solution.py
+++ b/solution.py
@@ -57,10 +57,8 @@
     sz,
     yp,
     yl,
-    gz,
-    gx,
-    gc,
-    gy,
+    ga,
+    gb,
     tile_sem,
     send_sem,
     left_sem,
@@ -106,12 +104,23 @@
         tile_copy(ch).start()
 
     barrier = pltpu.get_barrier_semaphore()
-    peers = (
-        [(row_of(z, i, core), c) for z in z_far]
-        + [(row_of(o, x, core), c) for x in x_far]
-        + [partner]
-        + [(r, y) for y in y_far]
-    )
+    near = [
+        ((i + d) % inner, (core + e) % 2, (i - d + inner) % inner)
+        for d in range(inner)
+        for e in range(2)
+        if d or e
+    ]
+    wide_set = [
+        ((o + d) % outer, (c + e) % n_c, (o - d + outer) % outer, (c - e + n_c) % n_c)
+        for d in range(outer)
+        for e in range(n_c)
+        if d or e
+    ]
+    near_peers = [(row_of(o, x, cc), c) for x, cc, _ in near]
+    near_src = [x * 2 + cc for _, cc, x in near]
+    wide_peers = [(row_of(z, i, core), y) for z, y, _, _ in wide_set]
+    wide_src = [z * n_c + y for _, _, z, y in wide_set]
+    peers = near_peers + wide_peers
     for peer in peers:
         pl.semaphore_signal(barrier, inc=1, device_id=peer, device_id_type=MESH)
     pl.semaphore_wait(barrier, len(peers))
@@ -231,8 +240,31 @@
             send(zp.at[at], zc.at[slot], zc_sem.at[slot], partner)
     relay_x()
     take_core()
-    for ch in range(chunks // 2):
-        images(ch, cv, col_s, block_cols, True)
+
+    def gram_step(p, total):
+        sums, mates = [], []
+        for t in range(piece):
+            high, low = split(zp[pl.ds(p * part + t * wide, vecs), :])
+            sums.append(jnp.concatenate([high, low], 0))
+            mates.append(cv[p * piece + t])
+        return total + mul(jnp.concatenate(sums, 1), jnp.concatenate(mates, 1), across)
+
+    total = lax.fori_loop(0, n_r, gram_step, jnp.zeros((2 * vecs, vecs), F32))
+
+    def spread(value, buf, base, me, far):
+        buf[me] = value
+        for peer in far:
+            send(buf.at[me], buf.at[me], g_sem.at[base + me], peer)
+
+    def collect(buf, base, src):
+        for q in src:
+            landed(buf.at[q], g_sem.at[base + q])
+        total = buf[0]
+        for q in range(1, buf.shape[0]):
+            total = total + buf[q]
+        return total
+
+    spread(total[:vecs] + total[vecs:], ga, 0, i * 2 + core, near_peers)
     def encode(block_of, q_ref, s_ref):
         scales = []
         for t in range(piece):
@@ -261,37 +293,15 @@
                 peer = (row_of(o, x, core), c)
                 send(qx_out.at[dx - 1, z], qx.at[dx - 1, z], zx_sem.at[dx - 1, z], peer)
                 send(sx_out.at[dx - 1, z], sx.at[dx - 1, z], sx_sem.at[dx - 1, z], peer)
+    for ch in range(chunks // 2):
+        images(ch, cv, col_s, block_cols, True)
+    spread(collect(ga, 0, near_src), gb, 2 * inner, o * n_c + c, wide_peers)
     for ch in range(chunks // 2, chunks):
         images(ch, cv, col_s, block_cols, True)
     gather_sums(row_v, block_rows, yp)
     for y in y_far:
         dy = (y - c + n_c) % n_c
         send(yp.at[pl.ds(y * part, part)], yl.at[dy], y_sem.at[dy], (r, y))
-
-    def gram_step(a, total):
-        at = pl.ds(a * wide, vecs)
-        high, low = split(yp[at, :])
-        mine = rv[a]
-        return total + mul(mine, high, across) + mul(mine, low, across)
-
-    gram = lax.fori_loop(0, block_rows, gram_step, jnp.zeros((vecs, vecs), F32))
-    used = 0
-
-    def spread(value, buf, me, far, src, peer):
-        nonlocal used
-        buf[me] = value
-        for f in far:
-            send(buf.at[me], buf.at[me], g_sem.at[used + me], peer(f))
-        for s in src:
-            landed(buf.at[s], g_sem.at[used + s])
-        used += buf.shape[0]
-        total = buf[0]
-        for q in range(1, buf.shape[0]):
-            total = total + buf[q]
-        return total
-
-    gram = spread(gram, gc, core, [1 - core], [1 - core], lambda f: (row_of(o, i, f), c))
-    gram = spread(gram, gx, i, x_far, x_src, lambda f: (row_of(o, f, core), c))
 
     def plane_sum(z, t):
         total = pair_sum(z, i, t)
@@ -312,8 +322,7 @@
             for t in range(piece):
                 zs[t * vecs : (t + 1) * vecs] = plane_sum(z, t)
 
-    gram = spread(gram, gy, c, y_far, y_src, lambda f: (r, f))
-    gram = spread(gram, gz, o, z_far, z_src, lambda f: (row_of(f, i, core), c))
+    gram = collect(gb, 2 * inner, wide_src)
     gram = gram * (block_cols * n_c * side) ** (-0.5)
     out_g[...] = gram
     y_total = yp[pl.ds(c * part, part), :]
@@ -371,10 +380,8 @@
             + planes
             + 2 * outer * (inner - 1)
             + 2 * (outer - 1)
-            + 1
-            + (inner - 1)
-            + (n_c - 1)
-            + (outer - 1)
+            + (2 * inner - 1)
+            + (outer * n_c - 1)
         )
         vmem = pl.BlockSpec(memory_space=pltpu.VMEM)
         smem = pl.BlockSpec(memory_space=pltpu.SMEM)
@@ -405,10 +412,8 @@
                 ],
                 pltpu.VMEM((block_rows * wide, side), F32),
                 pltpu.VMEM((n_c, part, side), F32),
-                pltpu.VMEM((outer, vecs, vecs), F32),
-                pltpu.VMEM((inner, vecs, vecs), F32),
-                pltpu.VMEM((2, vecs, vecs), F32),
-                pltpu.VMEM((n_c, vecs, vecs), F32),
+                pltpu.VMEM((2 * inner, vecs, vecs), F32),
+                pltpu.VMEM((outer * n_c, vecs, vecs), F32),
                 dma((chunks,)),
                 dma((sends,)),
                 dma((n_c,)),
@@ -416,7 +421,7 @@
                 dma((planes,)),
                 *[dma((near, outer)), dma((far,))] * 2,
                 dma((n_c,)),
-                dma((outer + inner + 2 + n_c,)),
+                dma((2 * inner + outer * n_c,)),
             ],
             compiler_params=pltpu.CompilerParams(
                 collective_id=0, has_side_effects=True, vmem_limit_bytes=60 * 1024 * 1024

time: 40.6 us -> 38 us (0.936)
  Pallas kernels: 39.8 us -> 37.2 us
    pallas_call x1, Pallas kernels: 37.9 us -> 35.2 us  [per_device(): pl.pallas_call(functools.partial(kernel, (n_r, n_c, outer, inner, chunks)...]
where the time goes in v4:
time: 38 us; the launch traced here: 37.8 us
  Pallas kernels  37.2 us (98%)
  between operations  0.64 us (2%)
    pallas_call x1, Pallas kernels, per_device(): pl.pallas_call(functools.partial(kernel, (n_r, n_c, outer, inner, chunks)...  35.2 us
    pallas_call x1, Pallas kernels, per_device(): pl.pallas_call(finish, out_shape=(jax.ShapeDtypeStruct((piece, vecs, side...  1.95 us

profile of v4, /device:TPU:0, one launch (start us, length us, event | category | flops | bytes accessed | tf_op | source)
XLA Modules:
  0.0 37.8 jit_solution(14670609294820086670)
XLA Ops:
  0.6 35.2 %arnoldi_step.1 = (f32[264,128]{1,0:T(8,128)}, f32[8,32,128]{2,1,0:T(8,128)}, f32[32,32]{1,0:T(8,128)}) custom-call(s32[256]{0:T(256)} %bitcast.4, s32[256]{0:T(256)} %bitcast.6, s32[1,256]{1,0:T(1,128)} %bitcast.5, s32[1,256]{1,0:T(1,128)} %bitcast.7, bf16[8,32,128]{2,1,0:T(8,128)(2,1)} %right.3, bf16[8,32,128]{2,1,0:T(8,128)(2,1)} %left.3, ...), custom_call_target="tpu_custom_call" | custom-call | tf_op jit(solution)/shard_map/arnoldi_step/pallas_call | solution.py:391
  35.8 2.0 %finish.1 = (f32[8,32,128]{2,1,0:T(8,128)}, f32[8,32,128]{2,1,0:T(8,128)}, f32[32,32]{1,0:T(8,128)}) custom-call(f32[264,128]{1,0:T(8,128)} %get-tuple-element.6.y_ref, f32[8,32,128]{2,1,0:T(8,128)} %get-tuple-element.7.z_ref, f32[32,32]{1,0:T(8,128)} %get-tuple-element.8.gram_ref, bf16[8,32,128]{2,1,0:T(8,128)(2,1)} %right.3, bf16[8,32,128]{2,1,0:T(8,128)(2,1)} %left.3), custom_call_target="tpu_custom_call" | custom-call | tf_op jit(solution)/shard_map/finish/pallas_call | solution.py:431
